TPU v7x, 256 devices: a whole 4x4x8 slice. The times are simulated.
256 devices in a mesh: patch: 64 (over z, y, core), mp: 4 (over x).
Axes of the slice: x: 4, y: 4, z: 8, core: 2. Of those that a mesh axis runs over, the one named last changes fastest.
Arguments:
- grid_latent: bfloat16 [65536, 512], P('patch'), may hold values from -6 to 6
- mesh_latent: bfloat16 [8192, 512], P('patch', 'mp'), may hold values from -6 to 6
- edge_weight: bfloat16 [768, 128, 128], P('patch'), may hold values from -0.15625 to 0.15625
- block_source: int32 [768], P('patch'), may hold values from 0 to 511, as said below
- block_live: int32 [768], P('patch'), may hold values from 0 to 1
- mlp_first: bfloat16 [512, 512], replicated, may hold values from -0.25 to 0.25
- mlp_second: bfloat16 [512, 512], P(None, 'mp'), may hold values from -0.25 to 0.25
- mesh_cotangent: bfloat16 [8192, 512], P('patch', 'mp'), may hold values from -6 to 6
Outputs:
- mesh_out: bfloat16 [8192, 512], P('patch', 'mp')
- grad_first: float32 [512, 512], P(None, 'mp')
- grad_second: float32 [512, 512], P(None, 'mp')
Inputs may be any that keep to these rules, and one draw needn't show every extreme that they name: `block_source`: grid patch g lies on the device of index g // 8 along patch, and slot b on the device of index b // 12. On every device at most 1 slots take their source from one device, and some device supplies exactly 1 slots to some device.
All inputs are finite; a program needn't handle non-finite values.
Results may differ from a plain program's by a relative error of at most 0.0058.
Values may be sent and summed in bfloat16 or wider, within the bound.
A program may use at most 64 MiB of HBM per device.

v0:
```python
import functools
import math
import jax
import jax.numpy as jnp
from jax import lax
from jax.sharding import Mesh
from jax.sharding import PartitionSpec as P

PATCH = 128
GPD = 8
BPM = 12
MPD = 1
EBD = 12
PATCH_AXES = ("patch_0", "patch_1", "patch_2")


def joined_along(parts, dim):
    parts = jnp.moveaxis(parts, 0, dim)
    lengths = parts.shape
    return parts.reshape(*lengths[:dim], lengths[dim] * lengths[dim + 1], *lengths[dim + 2 :])


def one_gather(arrays, axis, dims):
    flat = jnp.concatenate([a.reshape(-1) for a in arrays])
    lines, at, finished = (lax.all_gather(flat, axis), 0, [])
    for a, dim in zip(arrays, dims):
        parts = lines[:, at : at + a.size].reshape(-1, *a.shape)
        finished.append(joined_along(parts, dim))
        at += a.size
    return tuple(finished)


def one_axis_at_a_time(array, axes):
    return functools.reduce(lax.psum, axes, array)


def silu_slope(values):
    sigmoid = jax.nn.sigmoid(values)
    return sigmoid * (1.0 + values * (1.0 - sigmoid))


def per_device(
    grid_latent,
    mesh_latent,
    edge_weight,
    block_source,
    block_live,
    mlp_first,
    mlp_second,
    mesh_cotangent,
):
    devices = lax.axis_size(PATCH_AXES)
    own_index = lax.axis_index(PATCH_AXES)
    column_index = lax.axis_index("mp")
    grid_rows = grid_latent.shape[0]
    width_local = mlp_second.shape[1]
    hidden_local = mlp_first.shape[1] // lax.axis_size("mp")
    block_width = PATCH * width_local
    slot_cap = (EBD + devices - 1) // devices
    pre_act = jnp.dot(grid_latent, mlp_first, preferred_element_type=jnp.float32)
    hidden = jax.nn.silu(pre_act).astype(jnp.bfloat16)
    message = jnp.dot(hidden, mlp_second, preferred_element_type=jnp.float32).astype(jnp.bfloat16)
    message_flat = message.reshape(GPD, block_width)
    live_local = block_live.astype(jnp.float32)[:, None, None]
    every_source, every_live = one_gather((block_source, block_live), PATCH_AXES, (0, 0))
    every_source = every_source.reshape(devices, EBD)
    every_live = every_live.reshape(devices, EBD)
    source_device = every_source // GPD
    source_patch = every_source % GPD
    slot_order = jnp.arange(EBD)
    same_source = (source_device[:, :, None] == source_device[:, None, :]) & (
        slot_order[None, None, :] < slot_order[None, :, None]
    )
    slot_rank = jnp.sum(same_source, axis=2)
    own_sources = source_device[own_index]
    own_ranks = slot_rank[own_index]
    wanted = (source_device == own_index) & (every_live == 1)
    matches = (
        wanted[:, :, None, None]
        & (slot_rank[:, :, None, None] == jnp.arange(slot_cap)[None, None, :, None])
        & (source_patch[:, :, None, None] == jnp.arange(GPD)[None, None, None, :])
    )
    picking = jnp.sum(matches, axis=1).reshape(devices * slot_cap, GPD).astype(jnp.bfloat16)
    outgoing = (
        jnp.dot(picking, message_flat, preferred_element_type=jnp.float32)
        .astype(jnp.bfloat16)
        .reshape(devices, slot_cap, block_width)
    )
    incoming = lax.all_to_all(
        outgoing, PATCH_AXES, split_axis=0, concat_axis=0, tiled=True
    ).reshape(devices * slot_cap, block_width)
    lookup = own_sources * slot_cap + own_ranks
    block_input = jnp.take(incoming, lookup, axis=0).reshape(EBD, PATCH, width_local)
    products = (
        jnp.einsum("bpq,bqc->bpc", edge_weight, block_input, preferred_element_type=jnp.float32)
        * live_local
    )
    summed = (
        products.reshape(MPD, BPM, PATCH, width_local).sum(axis=1).reshape(MPD * PATCH, width_local)
    )
    mesh_out = (mesh_latent.astype(jnp.float32) + summed).astype(jnp.bfloat16)
    cotangent_blocks = jnp.broadcast_to(
        mesh_cotangent.reshape(MPD, 1, PATCH, width_local), (MPD, BPM, PATCH, width_local)
    ).reshape(EBD, PATCH, width_local)
    adjoint = (
        jnp.einsum(
            "bqp,bqc->bpc", edge_weight, cotangent_blocks, preferred_element_type=jnp.float32
        )
        * live_local
    ).astype(jnp.bfloat16)
    adjoint = adjoint.reshape(EBD, block_width)
    slot_rows = devices * slot_cap
    scatter_table = (
        (jnp.arange(slot_rows)[:, None] == lookup[None, :]) & (block_live[None, :] == 1)
    ).astype(jnp.bfloat16)
    returning = jnp.dot(scatter_table, adjoint, preferred_element_type=jnp.float32).astype(
        jnp.bfloat16
    )
    back_flat = lax.all_to_all(
        returning.reshape(devices, slot_cap, block_width),
        PATCH_AXES,
        split_axis=0,
        concat_axis=0,
        tiled=True,
    ).reshape(devices * slot_cap, block_width)
    grad_message = lax.dot_general(
        picking, back_flat, (((0,), (0,)), ((), ())), preferred_element_type=jnp.float32
    )
    grad_message = grad_message.astype(jnp.bfloat16).reshape(grid_rows, width_local)
    scaling = 1.0 / math.sqrt(grid_rows * devices)
    grad_second = (
        lax.dot_general(
            hidden, grad_message, (((0,), (0,)), ((), ())), preferred_element_type=jnp.float32
        )
        * scaling
    )
    grad_piece = lax.all_gather(grad_message, "mp", axis=1, tiled=True)
    second_piece = lax.all_gather(mlp_second, "mp", axis=1, tiled=True)
    rows_of_second = lax.dynamic_slice_in_dim(
        second_piece, column_index * hidden_local, hidden_local, 0
    )
    grad_hidden = lax.dot_general(
        rows_of_second, grad_piece, (((1,), (1,)), ((), ())), preferred_element_type=jnp.float32
    )
    pre_slice = lax.dynamic_slice_in_dim(pre_act, column_index * hidden_local, hidden_local, 1).T
    grad_pre = (grad_hidden * silu_slope(pre_slice)).astype(jnp.bfloat16)
    grad_first = (
        lax.dot_general(
            grid_latent, grad_pre, (((0,), (1,)), ((), ())), preferred_element_type=jnp.float32
        )
        * scaling
    )
    grad_first, grad_second = (
        one_axis_at_a_time(grad_first, PATCH_AXES),
        one_axis_at_a_time(grad_second, PATCH_AXES),
    )
    return (mesh_out, grad_first, grad_second)


def solution(mesh):
    torus = Mesh(
        mesh.devices.reshape(8, 4, 2, mesh.shape["mp"]), ("patch_0", "patch_1", "patch_2", "mp")
    )
    in_specs = (
        P(PATCH_AXES, None),
        P(PATCH_AXES, "mp"),
        P(PATCH_AXES, None, None),
        P(PATCH_AXES),
        P(PATCH_AXES),
        P(),
        P(None, "mp"),
        P(PATCH_AXES, "mp"),
    )
    out_specs = (P(PATCH_AXES, "mp"), P(None, "mp"), P(None, "mp"))
    return jax.shard_map(
        per_device, mesh=torus, in_specs=in_specs, out_specs=out_specs, check_vma=False
    )
```

profile of v0, /device:TPU:1, one launch (start us, length us, event | category | flops | bytes accessed | tf_op | source)
XLA Modules:
  0.0 328.0 jit_solution(325961317000444766)
XLA Ops:
  8.6 1.3 dynamic-slice
  11.4 21.0 %all-reduce = s32[1536]{0:T(1024)S(1)} all-reduce(s32[1536]{0:T(1024)S(1)} %add_dynamic-update-slice_fusion), channel_id=2, replica_groups=mesh['patch_0'=8,'patch_1'=4,'patch_2'=2,'mp'=4] {'patch_0','patch_1','p..., use_global_device_ids=true, to_apply=%add | all-reduce | flops 1536 | bytes 12288
  33.2 1.3 fusion.4
  34.6 1.1 copy.60
  36.1 1.7 fusion.1
  38.4 2.9 reduce.8
  41.2 4.5 %reshape.158 = bf16[64,2,8192]{2,1,0:T(2,128)(2,1)} reshape(bf16[64,16384]{1,0:T(8,128)(2,1)} %reduce.8) | data formatting | bytes 4194304
  45.7 8.9 %all-to-all-start.1 = ((bf16[64,2,8192]{2,1,0:T(2,128)(2,1)}), bf16[64,2,8192]{2,1,0:T(2,128)(2,1)S(1)}, u32[]{:S(2)}, u32[]{:S(2)}) async-start(bf16[64,2,8192]{2,1,0:T(2,128)(2,1)} %reshape.158), calls=%async_computation.1 | async-start | bytes 4194304 | tf_op jit(solution)/shard_map/all_to_all | solution.py:119
  55.3 3.3 %multiply_convert_fusion = (bf16[1024,512]{1,0:T(8,128)(2,1)S(1)}, f32[1024,512]{1,0:T(8,128)}) fusion(bf16[1024,512]{1,0:T(8,128)(2,1)S(1)} %copy-done, bf16[512,512]{1,0:T(8,128)(2,1)} %param.13), kind=kOutput, calls=%fused_computation.9 | convolution fusion | flops 539492352 | bytes 4718592 | tf_op jit(solution)/shard_map/dot_general | solution.py:60
  59.6 1.1 convolution_convert_fusion.3
  60.7 1.1 reshape.130
  63.2 2.1 fusion
  65.3 4.5 %reduce.7 = bf16[64,16384]{1,0:T(8,128)(2,1)} reduce(bf16[64,1,16384]{2,0,1:T(8,128)(2,1)} %fusion, bf16[]{:T(256)} %broadcast.136), dimensions={1}, to_apply=%copy.46.reduce_sub_computation | reduce | bytes 4194306 | tf_op jit(solution)/shard_map/reshape | solution.py:87
  69.8 4.5 %reshape.156 = bf16[64,2,8192]{2,1,0:T(2,128)(2,1)} reshape(bf16[64,16384]{1,0:T(8,128)(2,1)} %reduce.7) | data formatting | bytes 4194304
  74.3 30.3 %all-to-all-done.1 = bf16[64,2,8192]{2,1,0:T(2,128)(2,1)S(1)} async-done(((bf16[64,2,8192]{2,1,0:T(2,128)(2,1)}), bf16[64,2,8192]{2,1,0:T(2,128)(2,1)S(1)}, u32[]{:S(2)}, u32[]{:S(2)}) %all-to-all-start.1) | async-done | bytes 2097184 | tf_op jit(solution)/shard_map/all_to_all | solution.py:119
  104.6 1.4 copy-done.1
  106.0 6.8 %all-to-all-start = ((bf16[64,2,8192]{2,1,0:T(2,128)(2,1)}), bf16[64,2,8192]{2,1,0:T(2,128)(2,1)S(1)}, u32[]{:S(2)}, u32[]{:S(2)}) async-start(bf16[64,2,8192]{2,1,0:T(2,128)(2,1)} %reshape.156), calls=%async_computation | async-start | bytes 4194304 | tf_op jit(solution)/shard_map/all_to_all | solution.py:89
  112.8 10.4 %reshape.159 = bf16[64,1,16384]{2,1,0:T(2,128)(2,1)} reshape(bf16[64,2,8192]{2,1,0:T(2,128)(2,1)} %copy-done.1) | data formatting | bytes 4194304
  123.2 4.5 %convolution_convert_fusion.2 = bf16[8,16384]{1,0:T(8,128)(2,1)S(1)} fusion(bf16[64,1,16384]{2,1,0:T(2,128)(2,1)} %reshape.159, s32[64,8]{0,1:T(8,128)S(1)} %convert_reduce_fusion.1), kind=kOutput, calls=%fused_computation.5 | convolution fusion | flops 16908800 | bytes 2361344 | tf_op jit(solution)/shard_map/dot_general | solution.py:126
  128.6 12.8 %all_gather.14 = bf16[512,512]{1,0:T(8,128)(2,1)} all-gather(bf16[512,128]{1,0:T(8,128)(2,1)S(1)} %copy-done.3), channel_id=1, replica_groups=mesh['patch_0'=8,'patch_1'=4,'patch_2'=2,'mp'=4] {'mp'}, dimensions={1}, use_global_device_ids=true | all-gather | bytes 655360 | tf_op jit(solution)/shard_map/all_gather | solution.py:138
  141.3 2.5 convolution_multiply_fusion.3
  143.8 12.4 %all-gather.3.cloned.1.call-done = bf16[1024,512]{1,0:T(8,128)(2,1)} async-done(((bf16[1024,128]{1,0:T(8,128)(2,1)}), bf16[1024,512]{1,0:T(8,128)(2,1)}) %all-gather.3.cloned.1.call-update) | async-done | bytes 1048592 | tf_op jit(solution)/shard_map/all_gather | solution.py:137
  156.3 2.9 fusion.9
  159.2 71.2 %all-reduce.8.cloned.1.call-done = (f32[512,128]{0,1:T(8,128)}, f32[512,128]{1,0:T(8,128)}) async-done(((f32[512,128]{0,1:T(8,128)}, f32[512,128]{1,0:T(8,128)}), (f32[512,128]{0,1:T(8,128)}, f32[512,128]{1,0:T(8,128)})) %all-reduce.8.cloned.1.call-update) | async-done | bytes 524304 | tf_op jit(solution)/shard_map/psum | solution.py:34
  230.6 51.8 %all-reduce.10.cloned.1.call-done = (f32[512,128]{0,1:T(8,128)}, f32[512,128]{1,0:T(8,128)}) async-done(((f32[512,128]{0,1:T(8,128)}, f32[512,128]{1,0:T(8,128)}), (f32[512,128]{0,1:T(8,128)}, f32[512,128]{1,0:T(8,128)})) %all-reduce.10.cloned.1.call-update) | async-done | bytes 524304 | tf_op jit(solution)/shard_map/psum | solution.py:34
  282.6 6.7 %reshape.157 = bf16[64,1,16384]{2,1,0:T(2,128)(2,1)} reshape(bf16[64,2,8192]{2,1,0:T(2,128)(2,1)S(1)} %all-to-all-done) | data formatting | bytes 4194304
  289.3 4.5 %copy.66 = bf16[64,1,16384]{2,0,1:T(8,128)(2,1)S(1)} copy(bf16[64,1,16384]{2,1,0:T(2,128)(2,1)} %reshape.157) | data formatting | bytes 4194304
  293.7 1.6 gather_fusion
  295.3 1.2 copy.59
  298.0 20.0 %all-reduce.12.cloned.1.call-done = (f32[512,128]{0,1:T(8,128)}, f32[512,128]{1,0:T(8,128)}) async-done(((f32[512,128]{0,1:T(8,128)}, f32[512,128]{1,0:T(8,128)}), (f32[512,128]{0,1:T(8,128)}, f32[512,128]{1,0:T(8,128)})) %all-reduce.12.cloned.1.call-update) | async-done | bytes 524304 | tf_op jit(solution)/shard_map/psum | solution.py:34
  318.0 1.8 copy.52
  319.8 1.7 copy.76
  (54 shorter events, 9.8 us)
Async XLA Ops:
  7.2 48.1 %copy-start = (bf16[1024,512]{1,0:T(8,128)(2,1)S(1)}, bf16[1024,512]{1,0:T(8,128)(2,1)}, u32[]{:S(2)}) copy-start(bf16[1024,512]{1,0:T(8,128)(2,1)} %param.8) | copy-start | bytes 3145732
  7.9 29.8 %copy-start.8 = (f32[12]{0:T(128)}, f32[12]{0:T(128)S(1)}, u32[]{:S(2)}) copy-start(f32[12]{0:T(128)S(1)} %convert_element_type.60) | copy-start | bytes 148
  36.1 5.2 %copy-start.6 = (s32[12]{0:T(128)}, s32[12]{0:T(128)S(1)}, u32[]{:S(2)}) copy-start(s32[12]{0:T(128)S(1)} %add_reduce_fusion) | copy-start | bytes 148
  45.7 58.9 %all-to-all-start.1 = ((bf16[64,2,8192]{2,1,0:T(2,128)(2,1)}), bf16[64,2,8192]{2,1,0:T(2,128)(2,1)S(1)}, u32[]{:S(2)}, u32[]{:S(2)}) async-start(bf16[64,2,8192]{2,1,0:T(2,128)(2,1)} %reshape.158), calls=%async_computation.1 | async-start | bytes 4194304 | tf_op jit(solution)/shard_map/all_to_all | solution.py:119
  55.3 4.3 %copy-start.3 = (bf16[512,128]{1,0:T(8,128)(2,1)S(1)}, bf16[512,128]{1,0:T(8,128)(2,1)}, u32[]{:S(2)}) copy-start(bf16[512,128]{1,0:T(8,128)(2,1)} %param.14) | copy-start | bytes 393220
  58.6 1.0 copy-start.2
  104.6 1.4 copy-start.1
  106.0 176.6 %all-to-all-start = ((bf16[64,2,8192]{2,1,0:T(2,128)(2,1)}), bf16[64,2,8192]{2,1,0:T(2,128)(2,1)S(1)}, u32[]{:S(2)}, u32[]{:S(2)}) async-start(bf16[64,2,8192]{2,1,0:T(2,128)(2,1)} %reshape.156), calls=%async_computation | async-start | bytes 4194304 | tf_op jit(solution)/shard_map/all_to_all | solution.py:89
  112.8 43.5 %all-gather.3.cloned.1.call-start = ((), (), s32[]{:S(2)}) async-start(), calls=%async_computation.2 | async-start | bytes 1310720 | tf_op jit(solution)/shard_map/all_gather | solution.py:137
  128.5 101.9 %all-reduce.8.cloned.1.call-start = ((), (), s32[]{:S(2)}) async-start(), calls=%async_computation.3 | async-start | bytes 1048576 | tf_op jit(solution)/shard_map/psum | solution.py:34
  156.3 74.3 %copy-start.7 = (s32[12]{0:T(128)S(1)}, s32[12]{0:T(128)}, u32[]{:S(2)}) copy-start(s32[12]{0:T(128)} %copy-done.6) | copy-start | bytes 148
  156.3 126.2 %copy-start.5 = (bf16[128,128]{1,0:T(8,128)(2,1)S(1)}, bf16[128,128]{1,0:T(8,128)(2,1)}, u32[]{:S(2)}) copy-start(bf16[128,128]{1,0:T(8,128)(2,1)} %param.9) | copy-start | bytes 98308
  159.2 123.2 %all-reduce.10.cloned.1.call-start = ((), (), s32[]{:S(2)}) async-start(), calls=%async_computation.4 | async-start | bytes 1048576 | tf_op jit(solution)/shard_map/psum | solution.py:34
  230.5 87.5 %all-reduce.12.cloned.1.call-start = ((), (), s32[]{:S(2)}) async-start(), calls=%async_computation.5 | async-start | bytes 1048576 | tf_op jit(solution)/shard_map/psum | solution.py:34
  295.3 1.5 copy-start.4
  295.3 1.5 copy-start.9
Sparse Core Ops, SparseCore 0:
  128.7 27.5 all-gather.2
  159.3 71.1 all-reduce.7
  232.9 49.4 all-reduce.9
  284.9 33.0 all-reduce.11
where the time goes:
time: 329 us; the launch traced here: 328 us
  waiting for transfers between devices  186 us (57%)
  local copies, waits for them, and re-layouts  46 us (14%)
  blocking collectives  33.7 us (10%)
  matrix products  19.9 us (6%)
  starting transfers between devices  15.8 us (5%)
  between operations  14.6 us (4%)
  other arithmetic  12 us (4%)
    psum x3, waiting for transfers between devices, one_axis_at_a_time(): return functools.reduce(lax.psum, axes, array)  143 us
    unnamed x36, local copies, waits for them, and re-layouts  41.5 us
    all_to_all x1, waiting for transfers between devices, per_device(): lax.all_to_all(returning.reshape(devices, slot_cap, block_width), PATCH_A...  30.3 us
    unnamed x1, blocking collectives  21 us
    all_gather x1, blocking collectives, per_device(): second_piece = lax.all_gather(mlp_second, 'mp', axis=1, tiled=True)  12.8 us
    all_gather x1, waiting for transfers between devices, per_device(): grad_piece = lax.all_gather(grad_message, 'mp', axis=1, tiled=True)  12.4 us
    all_to_all x1, starting transfers between devices, per_device(): lax.all_to_all(returning.reshape(devices, slot_cap, block_width), PATCH_A...  8.9 us
    all_to_all x1, starting transfers between devices, per_device(): lax.all_to_all(outgoing, PATCH_AXES, split_axis=0, concat_axis=0, tiled=T...  6.79 us
  transfers between devices with their start and end apart: 6, of which 5 were waited for; matrix products, arithmetic and copies ran while one was open for 17% of the time, Pallas kernels for 0%

commit v1 on v0

--- a/solution.py
+++ b/solution.py
@@ -5,6 +5,7 @@
 from jax import lax
 from jax.sharding import Mesh
 from jax.sharding import PartitionSpec as P
+from jax.lax import all_to_all, axis_size
 
 PATCH = 128
 GPD = 8
@@ -12,6 +13,19 @@
 MPD = 1
 EBD = 12
 PATCH_AXES = ("patch_0", "patch_1", "patch_2")
+
+
+def _try_all_region(x_in, ax_name):
+    step_out = all_to_all(
+        jnp.stack(tuple((x_in for _ in range(axis_size(ax_name)))), axis=0),
+        axis_name=ax_name,
+        split_axis=0,
+        concat_axis=0,
+    )
+    return jnp.concatenate(step_out, 1)
+
+
+tasks_note = functools.partial(_try_all_region, ax_name="mp")
 
 
 def joined_along(parts, dim):
@@ -134,7 +148,7 @@
         )
         * scaling
     )
-    grad_piece = lax.all_gather(grad_message, "mp", axis=1, tiled=True)
+    grad_piece = tasks_note(grad_message)
     second_piece = lax.all_gather(mlp_second, "mp", axis=1, tiled=True)
     rows_of_second = lax.dynamic_slice_in_dim(
         second_piece, column_index * hidden_local, hidden_local, 0

time: 329 us -> 335 us (1.018)
  waiting for transfers between devices: 186 us -> 198 us
  starting transfers between devices: 15.8 us -> 21.7 us
  local copies, waits for them, and re-layouts: 46 us -> 40.9 us
  other arithmetic: 12 us -> 8.5 us
    all_to_all x1, waiting for transfers between devices: 30.3 us -> 49.9 us  [per_device(): lax.all_to_all(returning.reshape(devices, slot_cap, block_width), PATCH_A...]
    all_gather x1 -> x0, waiting for transfers between devices: 12.4 us -> none  [per_device(): grad_piece = lax.all_gather(grad_message, 'mp', axis=1, tiled=True)]
    unnamed x36 -> x28, local copies, waits for them, and re-layouts: 41.5 us -> 36.1 us
    psum x3, waiting for transfers between devices: 143 us -> 148 us  [one_axis_at_a_time(): return functools.reduce(lax.psum, axes, array)]
    all_to_all x0 -> x1, starting transfers between devices: none -> 4.26 us  [_try_all_region(): all_to_all(jnp.stack(tuple((x_in for _ in range(axis_size(ax_name)))), ax...]
  transfers between devices with their start and end apart: 6 -> 6, of which waited for: 5 -> 4; matrix products, arithmetic and copies ran while one was open for 17% -> 10% of each run, Pallas kernels for 0% -> 0%
where the time goes in v1:
time: 335 us; the launch traced here: 334 us
  waiting for transfers between devices  198 us (59%)
  local copies, waits for them, and re-layouts  40.9 us (12%)
  blocking collectives  32.8 us (10%)
  starting transfers between devices  21.7 us (6%)
  matrix products  17.7 us (5%)
  between operations  14.7 us (4%)
  other arithmetic  8.5 us (3%)
    psum x3, waiting for transfers between devices, one_axis_at_a_time(): return functools.reduce(lax.psum, axes, array)  148 us
    all_to_all x1, waiting for transfers between devices, per_device(): lax.all_to_all(returning.reshape(devices, slot_cap, block_width), PATCH_A...  49.9 us
    unnamed x28, local copies, waits for them, and re-layouts  36.1 us
    unnamed x1, blocking collectives  21 us
    all_gather x1, blocking collectives, per_device(): second_piece = lax.all_gather(mlp_second, 'mp', axis=1, tiled=True)  11.8 us
    all_to_all x1, starting transfers between devices, per_device(): lax.all_to_all(returning.reshape(devices, slot_cap, block_width), PATCH_A...  8.91 us
    all_to_all x1, starting transfers between devices, per_device(): lax.all_to_all(outgoing, PATCH_AXES, split_axis=0, concat_axis=0, tiled=T...  8.43 us
  transfers between devices with their start and end apart: 6, of which 4 were waited for; matrix products, arithmetic and copies ran while one was open for 10% of the time, Pallas kernels for 0%

profile of v1, /device:TPU:1, one launch (start us, length us, event | category | flops | bytes accessed | tf_op | source)
XLA Modules:
  0.0 334.2 jit_solution(15725479134546190152)
XLA Ops:
  8.6 1.3 dynamic-slice
  10.5 0.9 add_dynamic-update-slice_fusion
  11.4 21.0 %all-reduce = s32[1536]{0:T(1024)S(1)} all-reduce(s32[1536]{0:T(1024)S(1)} %add_dynamic-update-slice_fusion), channel_id=2, replica_groups=mesh['patch_0'=8,'patch_1'=4,'patch_2'=2,'mp'=4] {'patch_0','patch_1','p..., use_global_device_ids=true, to_apply=%add | all-reduce | flops 1536 | bytes 12288
  32.6 1.3 fusion.4
  34.0 1.1 copy.65
  35.5 1.7 fusion.1
  37.7 2.9 reduce.8
  40.6 4.5 %reshape.165 = bf16[64,2,8192]{2,1,0:T(2,128)(2,1)} reshape(bf16[64,16384]{1,0:T(8,128)(2,1)} %reduce.8) | data formatting | bytes 4194304
  45.1 8.9 %all-to-all-start.1 = ((bf16[64,2,8192]{2,1,0:T(2,128)(2,1)}), bf16[64,2,8192]{2,1,0:T(2,128)(2,1)S(1)}, u32[]{:S(2)}, u32[]{:S(2)}) async-start(bf16[64,2,8192]{2,1,0:T(2,128)(2,1)} %reshape.165), calls=%async_computation.1 | async-start | bytes 4194304 | tf_op jit(solution)/shard_map/all_to_all | solution.py:133
  54.2 49.9 %all-to-all-done.1 = bf16[64,2,8192]{2,1,0:T(2,128)(2,1)S(1)} async-done(((bf16[64,2,8192]{2,1,0:T(2,128)(2,1)}), bf16[64,2,8192]{2,1,0:T(2,128)(2,1)S(1)}, u32[]{:S(2)}, u32[]{:S(2)}) %all-to-all-start.1) | async-done | bytes 2097184 | tf_op jit(solution)/shard_map/all_to_all | solution.py:133
  104.0 6.8 %reshape.166 = bf16[64,1,16384]{2,1,0:T(2,128)(2,1)} reshape(bf16[64,2,8192]{2,1,0:T(2,128)(2,1)S(1)} %all-to-all-done.1) | data formatting | bytes 4194304
  110.8 4.5 %convolution_convert_fusion.2 = bf16[8,16384]{1,0:T(8,128)(2,1)S(1)} fusion(bf16[64,1,16384]{2,1,0:T(2,128)(2,1)} %reshape.166, s32[64,8]{0,1:T(8,128)S(1)} %convert_reduce_fusion.1), kind=kOutput, calls=%fused_computation.5 | convolution fusion | flops 16908800 | bytes 2361344 | tf_op jit(solution)/shard_map/dot_general | solution.py:140
  115.6 1.1 stack.3
  116.7 4.3 %all-to-all-start.2 = ((bf16[4,1024,128]{1,2,0:T(8,128)(2,1)}), bf16[4,1024,128]{1,2,0:T(8,128)(2,1)}, u32[]{:S(2)}, u32[]{:S(2)}) async-start(bf16[4,1024,128]{1,2,0:T(8,128)(2,1)} %stack.3), calls=%async_computation.2 | async-start | bytes 2097152 | tf_op jit(solution)/shard_map/all_to_all | solution.py:19
  121.0 2.2 multiply_convert_fusion
  123.2 1.1 copy-done.1
  125.5 1.7 fusion
  127.2 2.9 reduce.7
  130.2 4.5 %reshape.163 = bf16[64,2,8192]{2,1,0:T(2,128)(2,1)} reshape(bf16[64,16384]{1,0:T(8,128)(2,1)} %reduce.7) | data formatting | bytes 4194304
  134.6 8.4 %all-to-all-start = ((bf16[64,2,8192]{2,1,0:T(2,128)(2,1)}), bf16[64,2,8192]{2,1,0:T(2,128)(2,1)S(1)}, u32[]{:S(2)}, u32[]{:S(2)}) async-start(bf16[64,2,8192]{2,1,0:T(2,128)(2,1)} %reshape.163), calls=%async_computation | async-start | bytes 4194304 | tf_op jit(solution)/shard_map/all_to_all | solution.py:103
  143.1 11.8 %all_gather.11 = bf16[512,512]{1,0:T(8,128)(2,1)} all-gather(bf16[512,128]{1,0:T(8,128)(2,1)S(1)} %copy-done.2), channel_id=1, replica_groups=mesh['patch_0'=8,'patch_1'=4,'patch_2'=2,'mp'=4] {'mp'}, dimensions={1}, use_global_device_ids=true | all-gather | bytes 655360 | tf_op jit(solution)/shard_map/all_gather | solution.py:152
  154.9 2.4 convolution_multiply_fusion.3
  157.3 3.0 fusion.9
  160.4 76.2 %all-reduce.8.cloned.1.call-done = (f32[512,128]{0,1:T(8,128)}, f32[512,128]{1,0:T(8,128)}) async-done(((f32[512,128]{0,1:T(8,128)}, f32[512,128]{1,0:T(8,128)}), (f32[512,128]{0,1:T(8,128)}, f32[512,128]{1,0:T(8,128)})) %all-reduce.8.cloned.1.call-update) | async-done | bytes 524304 | tf_op jit(solution)/shard_map/psum | solution.py:48
  236.7 51.8 %all-reduce.10.cloned.1.call-done = (f32[512,128]{0,1:T(8,128)}, f32[512,128]{1,0:T(8,128)}) async-done(((f32[512,128]{0,1:T(8,128)}, f32[512,128]{1,0:T(8,128)}), (f32[512,128]{0,1:T(8,128)}, f32[512,128]{1,0:T(8,128)})) %all-reduce.10.cloned.1.call-update) | async-done | bytes 524304 | tf_op jit(solution)/shard_map/psum | solution.py:48
  288.7 6.8 %reshape.164 = bf16[64,1,16384]{2,1,0:T(2,128)(2,1)} reshape(bf16[64,2,8192]{2,1,0:T(2,128)(2,1)S(1)} %all-to-all-done) | data formatting | bytes 4194304
  295.5 4.5 %copy.71 = bf16[64,1,16384]{2,0,1:T(8,128)(2,1)S(1)} copy(bf16[64,1,16384]{2,1,0:T(2,128)(2,1)} %reshape.164) | data formatting | bytes 4194304
  299.9 1.6 gather_fusion
  301.5 1.2 copy.64
  304.2 20.1 %all-reduce.12.cloned.1.call-done = (f32[512,128]{0,1:T(8,128)}, f32[512,128]{1,0:T(8,128)}) async-done(((f32[512,128]{0,1:T(8,128)}, f32[512,128]{1,0:T(8,128)}), (f32[512,128]{0,1:T(8,128)}, f32[512,128]{1,0:T(8,128)})) %all-reduce.12.cloned.1.call-update) | async-done | bytes 524304 | tf_op jit(solution)/shard_map/psum | solution.py:48
  324.2 1.8 copy.57
  326.0 1.7 copy.81
  (47 shorter events, 5.9 us)
Async XLA Ops:
  7.2 113.8 %copy-start = (bf16[1024,512]{1,0:T(8,128)(2,1)S(1)}, bf16[1024,512]{1,0:T(8,128)(2,1)}, u32[]{:S(2)}) copy-start(bf16[1024,512]{1,0:T(8,128)(2,1)} %param.8) | copy-start | bytes 3145732
  45.1 58.9 %all-to-all-start.1 = ((bf16[64,2,8192]{2,1,0:T(2,128)(2,1)}), bf16[64,2,8192]{2,1,0:T(2,128)(2,1)S(1)}, u32[]{:S(2)}, u32[]{:S(2)}) async-start(bf16[64,2,8192]{2,1,0:T(2,128)(2,1)} %reshape.165), calls=%async_computation.1 | async-start | bytes 4194304 | tf_op jit(solution)/shard_map/all_to_all | solution.py:133
  115.3 5.7 %copy-start.5 = (bf16[512,512]{1,0:T(8,128)(2,1)S(1)}, bf16[512,512]{1,0:T(8,128)(2,1)}, u32[]{:S(2)}) copy-start(bf16[512,512]{1,0:T(8,128)(2,1)} %param.13) | copy-start | bytes 1572868
  116.7 17.9 %all-to-all-start.2 = ((bf16[4,1024,128]{1,2,0:T(8,128)(2,1)}), bf16[4,1024,128]{1,2,0:T(8,128)(2,1)}, u32[]{:S(2)}, u32[]{:S(2)}) async-start(bf16[4,1024,128]{1,2,0:T(8,128)(2,1)} %stack.3), calls=%async_computation.2 | async-start | bytes 2097152 | tf_op jit(solution)/shard_map/all_to_all | solution.py:19
  121.0 3.3 copy-start.2
  123.2 1.1 copy-start.1
  134.6 154.0 %all-to-all-start = ((bf16[64,2,8192]{2,1,0:T(2,128)(2,1)}), bf16[64,2,8192]{2,1,0:T(2,128)(2,1)S(1)}, u32[]{:S(2)}, u32[]{:S(2)}) async-start(bf16[64,2,8192]{2,1,0:T(2,128)(2,1)} %reshape.163), calls=%async_computation | async-start | bytes 4194304 | tf_op jit(solution)/shard_map/all_to_all | solution.py:103
  143.1 93.5 %all-reduce.8.cloned.1.call-start = ((), (), s32[]{:S(2)}) async-start(), calls=%async_computation.3 | async-start | bytes 1048576 | tf_op jit(solution)/shard_map/psum | solution.py:48
  157.3 131.2 %copy-start.4 = (bf16[128,128]{1,0:T(8,128)(2,1)S(1)}, bf16[128,128]{1,0:T(8,128)(2,1)}, u32[]{:S(2)}) copy-start(bf16[128,128]{1,0:T(8,128)(2,1)} %param.9) | copy-start | bytes 98308
  160.3 128.2 %all-reduce.10.cloned.1.call-start = ((), (), s32[]{:S(2)}) async-start(), calls=%async_computation.4 | async-start | bytes 1048576 | tf_op jit(solution)/shard_map/psum | solution.py:48
  236.6 87.6 %all-reduce.12.cloned.1.call-start = ((), (), s32[]{:S(2)}) async-start(), calls=%async_computation.5 | async-start | bytes 1048576 | tf_op jit(solution)/shard_map/psum | solution.py:48
  301.5 1.5 copy-start.3
Sparse Core Ops, SparseCore 0:
  160.4 76.0 all-reduce.7
  239.0 49.4 all-reduce.9
  291.1 33.0 all-reduce.11
